TPU v7x, 512 devices: a whole 4x4x16 slice. The times are simulated.
512 devices in a mesh: ctx: 32 (over z_lo, x, core), head: 16 (over y, z_hi).
Axes of the slice: x: 4, y: 4, z: 16 (z_hi: 4, z_lo: 4; z = z_hi * 4 + z_lo), core: 2. Of those that a mesh axis runs over, the one named last changes fastest.
Arguments:
- hidden_in: bfloat16 [4096, 4096], P('ctx', 'head'), may hold values from -6 to 6
- queries: bfloat16 [4096, 4096], P('ctx', 'head'), may hold values from -16 to 16
- kv_prev: bfloat16 [4096, 2, 4096], P('ctx', None, 'head'), may hold values from -16 to 16
- norm_gain: bfloat16 [4096], replicated, may hold values from 0.099609375 to 1.8984375
- w_kv: bfloat16 [4096, 2, 4096], P(None, None, 'head'), may hold values from -0.09375 to 0.09375
- w_out: bfloat16 [4096, 4096], P('head', 'ctx'), may hold values from -0.1875 to 0.1875
Outputs:
- hidden_out: float32 [4096, 4096], P('ctx', 'head')
- kv_out: float32 [4096, 2, 4096], P('ctx', None, 'head')
All inputs are finite; a program needn't handle non-finite values.
Results may differ from a plain program's by a relative error of at most 0.033.
Values may be sent and summed in bfloat16 or wider, within the bound.
No kernel may reach another device: no remote copies, remote signals or barrier semaphores. Data moves between devices by JAX's collectives and lax.ppermute only.
A program may use at most 64 MiB of HBM per device.

v0:
```python
import jax
import jax.numpy as jnp
from jax import lax
from jax.sharding import PartitionSpec as P

D = 4096
HD = 128
ITERS = 2
MASKED = -1e30
EPSILON = 1e-05


def attend_keys(query_heads, key_value, row_start):
    row_count = query_heads.shape[0]
    head_count = query_heads.shape[1]
    score_scale = HD ** (-0.5)
    query_position = row_start + jnp.arange(row_count)
    row_last = row_start + row_count - 1
    initial = (
        jnp.full((row_count, head_count), MASKED, jnp.float32),
        jnp.zeros((row_count, head_count), jnp.float32),
        jnp.zeros((row_count, head_count, HD), jnp.float32),
    )
    incoming = lax.all_gather(key_value, "ctx", axis=0, tiled=True)

    def advance(current):
        row_max, row_sum, weighted = current
        block_rows = incoming.shape[0]
        key_block = incoming[:, 0].reshape(block_rows, head_count, HD)
        value_block = incoming[:, 1].reshape(block_rows, head_count, HD)
        scores = (
            jnp.einsum("qhd,khd->qhk", query_heads, key_block, preferred_element_type=jnp.float32)
            * score_scale
        )
        allowed = (query_position[:, None] >= jnp.arange(block_rows)[None, :])[:, None, :]
        scores = jnp.where(allowed, scores, MASKED)
        new_max = jnp.maximum(row_max, jnp.max(scores, axis=2))
        weights = jnp.where(allowed, jnp.exp(scores - new_max[:, :, None]), 0.0)
        row_sum = jnp.sum(weights, axis=2)
        weighted = jnp.einsum(
            "qhk,khd->qhd",
            weights.astype(jnp.bfloat16),
            value_block,
            preferred_element_type=jnp.float32,
        )
        return (new_max, row_sum, weighted)

    row_max, row_sum, weighted = lax.cond(
        jnp.int32(0) <= row_last, advance, lambda current: current, initial
    )
    return (weighted / row_sum[:, :, None]).astype(jnp.bfloat16).reshape(row_count, head_count * HD)


def per_device(hidden_in, queries, kv_prev, norm_gain, w_kv, w_out):
    row_count = queries.shape[0]
    local_width = queries.shape[1]
    head_count = local_width // HD
    row_start = lax.axis_index("ctx") * row_count
    column_start = lax.axis_index("head") * local_width
    out_rows = lax.all_gather(w_out, "ctx", axis=1, tiled=True)
    kv_weights = w_kv.reshape(w_kv.shape[0], 2 * local_width)
    gain_all = norm_gain.astype(jnp.float32)
    gain_here = lax.dynamic_slice_in_dim(gain_all, column_start, local_width)
    query_heads = queries.reshape(row_count, head_count, HD)
    input_here = hidden_in.astype(jnp.float32)
    key_value = kv_prev
    for iteration in range(ITERS):
        attended = attend_keys(query_heads, key_value, row_start)
        partial_value = jnp.dot(attended, out_rows, preferred_element_type=jnp.float32)
        branch_sum = lax.psum_scatter(
            partial_value.astype(jnp.bfloat16), "head", scatter_dimension=1, tiled=True
        ).astype(jnp.float32)
        hidden = input_here + branch_sum
        squares = lax.psum(jnp.sum(hidden * hidden, axis=1), "head")
        normed = (hidden * lax.rsqrt(squares / D + EPSILON)[:, None] * gain_here).astype(
            jnp.bfloat16
        )
        fresh_kv = jnp.dot(
            lax.all_gather(normed, "head", axis=1, tiled=True),
            kv_weights,
            preferred_element_type=jnp.float32,
        )
        hidden_out = hidden
        kv_product = fresh_kv.reshape(row_count, 2, local_width)
        key_value = kv_product.astype(jnp.bfloat16)
    return (hidden_out, kv_product)


def solution(mesh):
    in_specs = (
        P("ctx", "head"),
        P("ctx", "head"),
        P("ctx", None, "head"),
        P(),
        P(None, None, "head"),
        P("head", "ctx"),
    )
    out_specs = (P("ctx", "head"), P("ctx", None, "head"))
    return jax.shard_map(
        per_device, mesh=mesh, in_specs=in_specs, out_specs=out_specs, check_vma=False
    )
```

profile of v0, /device:TPU:97, one launch (start us, length us, event | category | flops | bytes accessed | tf_op | source)
XLA Modules:
  0.0 747.0 jit_solution(11621251483294013254)
XLA Ops:
  7.2 1.7 copy.38
  9.7 1.0 copy.39
  10.7 77.8 %all-gather.6.cloned.1.call-done = bf16[4096,2,256]{0,2,1:T(8,128)(2,1)} async-done(((bf16[128,2,256]{0,2,1:T(8,128)(2,1)}), bf16[4096,2,256]{0,2,1:T(8,128)(2,1)}) %all-gather.6.cloned.1.call-update) | async-done | bytes 4194320 | tf_op jit(solution)/shard_map/all_gather | solution.py:24
  88.5 6.9 conditional.2
  88.9 2.7 fusion.29
  91.6 1.3 fusion.30
  92.9 1.5 fusion.9
  94.5 0.8 fusion.3
  95.4 62.8 %all-gather.8.cloned.1.call-done = bf16[256,4096]{1,0:T(8,128)(2,1)} async-done(((bf16[256,128]{1,0:T(8,128)(2,1)}), bf16[256,4096]{1,0:T(8,128)(2,1)}) %all-gather.8.cloned.1.call-update) | async-done | bytes 2097168 | tf_op jit(solution)/shard_map/all_gather | solution.py:60
  158.3 3.0 convolution_convert_fusion.1
  162.1 110.8 %reduce-scatter.3.cloned.1.call-done = bf16[128,256]{1,0:T(8,128)(2,1)} async-done(((bf16[128,4096]{1,0:T(8,128)(2,1)}), bf16[128,256]{1,0:T(8,128)(2,1)}) %reduce-scatter.3.cloned.1.call-update) | async-done | bytes 65552 | tf_op jit(solution)/shard_map/reduce_scatter | solution.py:70
  272.9 0.9 multiply_reduce_fusion.1
  273.9 44.0 %psum.14 = f32[128]{0:T(128)S(1)} all-reduce(f32[128]{0:T(128)S(1)} %multiply_reduce_fusion.1), channel_id=1, replica_groups=mesh['ctx'=32,'head'=16] {'head'}, use_global_device_ids=true, to_apply=%region_6.7 | all-reduce | flops 128 | bytes 1024 | tf_op jit(solution)/shard_map/psum | solution.py:74
  317.9 1.6 multiply_convert_fusion.1
  319.5 4.9 copy.59
  324.4 6.4 copy.42
  330.8 78.9 %all-gather.10.cloned.1.call-done = bf16[128,4096]{1,0:T(8,128)(2,1)} async-done(((bf16[128,256]{1,0:T(8,128)(2,1)}), bf16[128,4096]{1,0:T(8,128)(2,1)}) %all-gather.10.cloned.1.call-update) | async-done | bytes 1048592 | tf_op jit(solution)/shard_map/all_gather | solution.py:79
  409.7 4.7 convolution_convert_fusion.2
  414.6 59.2 %all-gather.12.cloned.1.call-done = bf16[4096,2,256]{2,0,1:T(8,128)(2,1)} async-done(((bf16[128,2,256]{2,0,1:T(8,128)(2,1)}), bf16[4096,2,256]{2,0,1:T(8,128)(2,1)}) %all-gather.12.cloned.1.call-update) | async-done | bytes 4194320 | tf_op jit(solution)/shard_map/all_gather | solution.py:24
  473.8 13.5 %conditional.3 = (f32[128,2]{0,1:T(2,128)S(1)}, f32[128,2,128]{0,2,1:T(8,128)S(1)}) conditional(s32[]{:T(128)} %convert_element_type.44, () %tuple.24, (s32[128]{0:T(128)S(1)}, bf16[4096,2,256]{2,0,1:T(8,128)(2,1)}, bf16[128,2,128]{0,2,1:T(8,128)(2,1)S(1)}) %tuple.65), branch_computations={%region_7.8_spmd, %region_8.11_spmd} | conditional | flops 546832128 | bytes 36117008 | solution.py:48
  474.2 6.6 copy.43
  480.8 2.7 fusion.31
  483.5 1.3 fusion.32
  484.8 1.5 fusion.22
  486.3 0.8 fusion.16
  487.3 1.4 convolution_convert_fusion
  488.9 110.3 %reduce-scatter.5.cloned.1.call-done = bf16[128,256]{1,0:T(8,128)(2,1)} async-done(((bf16[128,4096]{1,0:T(8,128)(2,1)}), bf16[128,256]{1,0:T(8,128)(2,1)}) %reduce-scatter.5.cloned.1.call-update) | async-done | bytes 65552 | tf_op jit(solution)/shard_map/reduce_scatter | solution.py:70
  599.2 0.9 multiply_reduce_fusion
  600.1 44.1 %psum.15 = f32[128]{0:T(128)S(1)} all-reduce(f32[128]{0:T(128)S(1)} %get-tuple-element.51), channel_id=1, replica_groups=mesh['ctx'=32,'head'=16] {'head'}, use_global_device_ids=true, to_apply=%region_13.14 | all-reduce | flops 128 | bytes 1024 | tf_op jit(solution)/shard_map/psum | solution.py:74
  644.9 90.2 %all-gather.14.cloned.1.call-done = bf16[128,4096]{1,0:T(8,128)(2,1)} async-done(((bf16[128,256]{1,0:T(8,128)(2,1)}), bf16[128,4096]{1,0:T(8,128)(2,1)}) %all-gather.14.cloned.1.call-update) | async-done | bytes 1048592 | tf_op jit(solution)/shard_map/all_gather | solution.py:79
  735.1 4.0 fusion.26
  739.2 0.9 copy.46
  (33 shorter events, 3.7 us)
Async XLA Ops:
  7.2 81.4 %all-gather.6.cloned.1.call-start = ((), (), s32[]{:S(2)}) async-start(), calls=%async_computation.2 | async-start | bytes 4325376 | tf_op jit(solution)/shard_map/all_gather | solution.py:24
  8.9 149.4 %all-gather.8.cloned.1.call-start = ((), (), s32[]{:S(2)}) async-start(), calls=%async_computation.3 | async-start | bytes 2162688 | tf_op jit(solution)/shard_map/all_gather | solution.py:60
  9.7 263.2 %reduce-scatter.3.cloned.1.call-start = ((), (), s32[]{:S(2)}) async-start(), calls=%async_computation.4 | async-start | bytes 1114112 | tf_op jit(solution)/shard_map/reduce_scatter | solution.py:70
  95.4 177.5 %copy-start.1 = (bf16[128,256]{1,0:T(8,128)(2,1)S(1)}, bf16[128,256]{1,0:T(8,128)(2,1)}, u32[]{:S(2)}) copy-start(bf16[128,256]{1,0:T(8,128)(2,1)} %param.10) | copy-start | bytes 196612
  161.3 248.3 %all-gather.10.cloned.1.call-start = ((), (), s32[]{:S(2)}) async-start(), calls=%async_computation.5 | async-start | bytes 1114112 | tf_op jit(solution)/shard_map/all_gather | solution.py:79
  319.5 154.4 %all-gather.12.cloned.1.call-start = ((), (), s32[]{:S(2)}) async-start(), calls=%async_computation.6 | async-start | bytes 4325376 | tf_op jit(solution)/shard_map/all_gather | solution.py:24
  414.4 184.8 %reduce-scatter.5.cloned.1.call-start = ((), (), s32[]{:S(2)}) async-start(), calls=%async_computation.7 | async-start | bytes 1114112 | tf_op jit(solution)/shard_map/reduce_scatter | solution.py:70
  473.8 13.5 %copy-start = (bf16[256,4096]{1,0:T(8,128)(2,1)S(1)}, bf16[256,4096]{1,0:T(8,128)(2,1)}, u32[]{:S(2)}) copy-start(bf16[256,4096]{1,0:T(8,128)(2,1)} %all-gather.8.cloned.1.call-done) | copy-start | bytes 6291460
  488.8 246.3 %all-gather.14.cloned.1.call-start = ((), (), s32[]{:S(2)}) async-start(), calls=%async_computation.8 | async-start | bytes 1114112 | tf_op jit(solution)/shard_map/all_gather | solution.py:79
  600.1 140.0 %copy-start.2 = (f32[128,256]{1,0:T(8,128)}, f32[128,256]{1,0:T(8,128)S(1)}, u32[]{:S(2)}) copy-start(f32[128,256]{1,0:T(8,128)S(1)} %get-tuple-element.52) | copy-start | bytes 393220
Sparse Core Ops, SparseCore 0:
  10.6 77.8 all-gather.5
  90.6 67.6 all-gather.7
  162.4 110.4 reduce-scatter.2
  319.6 90.0 all-gather.9
  414.5 59.2 all-gather.11
  488.9 110.1 reduce-scatter.4
  645.1 90.0 all-gather.13
where the time goes:
time: 748 us; the launch traced here: 747 us
  waiting for transfers between devices  591 us (79%)
  blocking collectives  88.1 us (12%)
  local copies, waits for them, and re-layouts  27 us (4%)
  matrix products  18.9 us (3%)
  between operations  14.2 us (2%)
    reduce_scatter x2, waiting for transfers between devices, per_device(): lax.psum_scatter(partial_value.astype(jnp.bfloat16), 'head', scatter_dime...  221 us
    all_gather x2, waiting for transfers between devices, per_device(): lax.all_gather(normed, 'head', axis=1, tiled=True)  169 us
    all_gather x2, waiting for transfers between devices, attend_keys(): incoming = lax.all_gather(key_value, 'ctx', axis=0, tiled=True)  137 us
    psum x2, blocking collectives, per_device(): squares = lax.psum(jnp.sum(hidden * hidden, axis=1), 'head')  88.1 us
    all_gather x1, waiting for transfers between devices, per_device(): out_rows = lax.all_gather(w_out, 'ctx', axis=1, tiled=True)  62.8 us
  transfers between devices with their start and end apart: 7, of which 7 were waited for; matrix products, arithmetic and copies ran while one was open for 3% of the time, Pallas kernels for 0%

commit v1 on v0

--- a/solution.py
+++ b/solution.py
@@ -75,10 +75,20 @@
         normed = (hidden * lax.rsqrt(squares / D + EPSILON)[:, None] * gain_here).astype(
             jnp.bfloat16
         )
+
+        def wait_quarters_on_mesh(xin, array_axis):
+            return jnp.concatenate(
+                jax.lax.all_to_all(
+                    jnp.stack([xin] * jax.lax.axis_size("head")),
+                    axis_name="head",
+                    split_axis=0,
+                    concat_axis=0,
+                ),
+                array_axis,
+            )
+
         fresh_kv = jnp.dot(
-            lax.all_gather(normed, "head", axis=1, tiled=True),
-            kv_weights,
-            preferred_element_type=jnp.float32,
+            wait_quarters_on_mesh(normed, 1), kv_weights, preferred_element_type=jnp.float32
         )
         hidden_out = hidden
         kv_product = fresh_kv.reshape(row_count, 2, local_width)

time: 748 us -> 694 us (0.928)
  the two profiles are of different devices: /device:TPU:97 before, /device:TPU:4 now
where the time goes in v1:
time: 694 us; the launch traced here: 693 us
  waiting for transfers between devices  466 us (67%)
  blocking collectives  154 us (22%)
  local copies, waits for them, and re-layouts  30.5 us (4%)
  matrix products  18.3 us (3%)
  between operations  13.9 us (2%)
    reduce_scatter x2, waiting for transfers between devices, per_device(): lax.psum_scatter(partial_value.astype(jnp.bfloat16), 'head', scatter_dime...  231 us
    all_gather x2, waiting for transfers between devices, attend_keys(): incoming = lax.all_gather(key_value, 'ctx', axis=0, tiled=True)  137 us
    psum x2, blocking collectives, per_device(): squares = lax.psum(jnp.sum(hidden * hidden, axis=1), 'head')  104 us
    all_gather x1, waiting for transfers between devices, per_device(): out_rows = lax.all_gather(w_out, 'ctx', axis=1, tiled=True)  62.8 us
    all_to_all x1, blocking collectives, wait_quarters_on_mesh(): jax.lax.all_to_all(jnp.stack([xin] * jax.lax.axis_size('head')), axis_nam...  50.2 us
    all_to_all x1, waiting for transfers between devices, wait_quarters_on_mesh(): jax.lax.all_to_all(jnp.stack([xin] * jax.lax.axis_size('head')), axis_nam...  34.5 us
  transfers between devices with their start and end apart: 6, of which 6 were waited for; matrix products, arithmetic and copies ran while one was open for 3% of the time, Pallas kernels for 0%

profile of v1, /device:TPU:4, one launch (start us, length us, event | category | flops | bytes accessed | tf_op | source)
XLA Modules:
  0.0 693.4 jit_solution(10020664413431481304)
XLA Ops:
  7.2 1.7 copy.38
  9.7 1.0 copy.39
  10.7 79.1 %all-gather.4.cloned.1.call-done = bf16[4096,2,256]{0,2,1:T(8,128)(2,1)} async-done(((bf16[128,2,256]{0,2,1:T(8,128)(2,1)}), bf16[4096,2,256]{0,2,1:T(8,128)(2,1)}) %all-gather.4.cloned.1.call-update) | async-done | bytes 4194320 | tf_op jit(solution)/shard_map/all_gather | solution.py:24
  89.8 6.9 conditional.2
  90.1 2.7 fusion.26
  92.9 1.3 fusion.27
  94.2 1.5 fusion.9
  96.7 62.8 %all-gather.6.cloned.1.call-done = bf16[256,4096]{1,0:T(8,128)(2,1)} async-done(((bf16[256,128]{1,0:T(8,128)(2,1)}), bf16[256,4096]{1,0:T(8,128)(2,1)}) %all-gather.6.cloned.1.call-update) | async-done | bytes 2097168 | tf_op jit(solution)/shard_map/all_gather | solution.py:60
  159.5 3.1 convolution_convert_fusion.1
  163.4 115.5 %reduce-scatter.3.cloned.1.call-done = bf16[128,256]{1,0:T(8,128)(2,1)} async-done(((bf16[128,4096]{1,0:T(8,128)(2,1)}), bf16[128,256]{1,0:T(8,128)(2,1)}) %reduce-scatter.3.cloned.1.call-update) | async-done | bytes 65552 | tf_op jit(solution)/shard_map/reduce_scatter | solution.py:70
  278.9 0.9 multiply_reduce_fusion.1
  279.8 51.7 %psum.14 = f32[128]{0:T(128)S(1)} all-reduce(f32[128]{0:T(128)S(1)} %multiply_reduce_fusion.1), channel_id=1, replica_groups=mesh['ctx'=32,'head'=16] {'head'}, use_global_device_ids=true, to_apply=%region_6.7 | all-reduce | flops 128 | bytes 1024 | tf_op jit(solution)/shard_map/psum | solution.py:74
  331.5 0.9 multiply_convert_fusion.1
  332.5 1.2 stack.4
  333.6 4.7 all-to-all-start
  338.4 4.9 copy.61
  343.2 6.4 copy.43
  349.7 34.5 %all-to-all-done = bf16[16,128,256]{2,1,0:T(8,128)(2,1)S(1)} async-done(((bf16[16,128,256]{2,1,0:T(8,128)(2,1)}), bf16[16,128,256]{2,1,0:T(8,128)(2,1)S(1)}, u32[]{:S(2)}, u32[]{:S(2)}) %all-to-all-start) | async-done | bytes 1048608 | tf_op jit(solution)/shard_map/all_to_all | solution.py:81
  385.3 4.4 convolution_convert_fusion.2
  389.9 57.9 %all-gather.8.cloned.1.call-done = bf16[4096,2,256]{2,0,1:T(8,128)(2,1)} async-done(((bf16[128,2,256]{2,0,1:T(8,128)(2,1)}), bf16[4096,2,256]{2,0,1:T(8,128)(2,1)}) %all-gather.8.cloned.1.call-update) | async-done | bytes 4194320 | tf_op jit(solution)/shard_map/all_gather | solution.py:24
  447.8 13.5 %conditional.3 = (f32[128,2]{0,1:T(2,128)S(1)}, f32[128,2,128]{0,2,1:T(8,128)S(1)}) conditional(s32[]{:T(128)} %convert_element_type.44, () %tuple.24, (s32[128]{0:T(128)S(1)}, bf16[4096,2,256]{2,0,1:T(8,128)(2,1)}, bf16[128,2,128]{0,2,1:T(8,128)(2,1)S(1)}) %tuple.61), branch_computations={%region_7.8_spmd, %region_8.11_spmd} | conditional | flops 546832128 | bytes 36117008 | solution.py:48
  448.1 6.6 copy.44
  454.7 2.7 fusion.28
  457.5 1.3 fusion.29
  458.8 1.5 fusion.22
  461.3 1.4 convolution_convert_fusion
  462.8 115.1 %reduce-scatter.5.cloned.1.call-done = bf16[128,256]{1,0:T(8,128)(2,1)} async-done(((bf16[128,4096]{1,0:T(8,128)(2,1)}), bf16[128,256]{1,0:T(8,128)(2,1)}) %reduce-scatter.5.cloned.1.call-update) | async-done | bytes 65552 | tf_op jit(solution)/shard_map/reduce_scatter | solution.py:70
  577.9 0.9 multiply_reduce_fusion
  578.9 51.8 %psum.15 = f32[128]{0:T(128)S(1)} all-reduce(f32[128]{0:T(128)S(1)} %get-tuple-element.51), channel_id=1, replica_groups=mesh['ctx'=32,'head'=16] {'head'}, use_global_device_ids=true, to_apply=%region_13.14 | all-reduce | flops 128 | bytes 1024 | tf_op jit(solution)/shard_map/psum | solution.py:74
  630.9 50.2 %all_to_all.10 = bf16[16,128,256]{2,1,0:T(8,128)(2,1)S(1)} all-to-all(bf16[16,128,256]{2,1,0:T(8,128)(2,1)S(1)} %stack.5), channel_id=1, replica_groups=mesh['ctx'=32,'head'=16] {'head'}, dimensions={0} | all-to-all | bytes 2097152 | tf_op jit(solution)/shard_map/all_to_all | solution.py:81
  682.2 3.7 fusion.30
  686.0 0.9 copy.48
  (36 shorter events, 7.0 us)
Async XLA Ops:
  7.2 82.6 %all-gather.4.cloned.1.call-start = ((), (), s32[]{:S(2)}) async-start(), calls=%async_computation.4 | async-start | bytes 4325376 | tf_op jit(solution)/shard_map/all_gather | solution.py:24
  8.9 150.6 %all-gather.6.cloned.1.call-start = ((), (), s32[]{:S(2)}) async-start(), calls=%async_computation.5 | async-start | bytes 2162688 | tf_op jit(solution)/shard_map/all_gather | solution.py:60
  9.7 269.2 %reduce-scatter.3.cloned.1.call-start = ((), (), s32[]{:S(2)}) async-start(), calls=%async_computation.6 | async-start | bytes 1114112 | tf_op jit(solution)/shard_map/reduce_scatter | solution.py:70
  96.7 182.2 %copy-start.1 = (bf16[128,256]{1,0:T(8,128)(2,1)S(1)}, bf16[128,256]{1,0:T(8,128)(2,1)}, u32[]{:S(2)}) copy-start(bf16[128,256]{1,0:T(8,128)(2,1)} %param.10) | copy-start | bytes 196612
  333.6 50.5 %all-to-all-start = ((bf16[16,128,256]{2,1,0:T(8,128)(2,1)}), bf16[16,128,256]{2,1,0:T(8,128)(2,1)S(1)}, u32[]{:S(2)}, u32[]{:S(2)}) async-start(bf16[16,128,256]{2,1,0:T(8,128)(2,1)} %stack.4), calls=%async_computation.1 | async-start | bytes 2097152 | tf_op jit(solution)/shard_map/all_to_all | solution.py:81
  338.3 109.5 %all-gather.8.cloned.1.call-start = ((), (), s32[]{:S(2)}) async-start(), calls=%async_computation.7 | async-start | bytes 4325376 | tf_op jit(solution)/shard_map/all_gather | solution.py:24
  389.7 188.3 %reduce-scatter.5.cloned.1.call-start = ((), (), s32[]{:S(2)}) async-start(), calls=%async_computation.8 | async-start | bytes 1114112 | tf_op jit(solution)/shard_map/reduce_scatter | solution.py:70
  447.8 13.5 %copy-start = (bf16[256,4096]{1,0:T(8,128)(2,1)S(1)}, bf16[256,4096]{1,0:T(8,128)(2,1)}, u32[]{:S(2)}) copy-start(bf16[256,4096]{1,0:T(8,128)(2,1)} %all-gather.6.cloned.1.call-done) | copy-start | bytes 6291460
  578.9 107.1 %copy-start.2 = (f32[128,256]{1,0:T(8,128)}, f32[128,256]{1,0:T(8,128)S(1)}, u32[]{:S(2)}) copy-start(f32[128,256]{1,0:T(8,128)S(1)} %get-tuple-element.52) | copy-start | bytes 393220
Sparse Core Ops, SparseCore 0:
  10.6 79.1 all-gather.3
  91.9 67.6 all-gather.5
  163.6 115.1 reduce-scatter.2
  389.8 57.9 all-gather.7
  462.9 114.9 reduce-scatter.4
